TPU v7x, 32 devices: a whole 2x2x4 slice. The times are simulated.
32 devices in a mesh: fsdp: 16 (over z, y, core), seq: 2 (over x).
Axes of the slice: x: 2, y: 2, z: 4, core: 2. Of those that a mesh axis runs over, the one named last changes fastest.
Arguments:
- block_input: bfloat16 [2, 16, 1024, 1024], P(None, 'fsdp', 'seq'), may hold values from -6 to 6
- output_grad: bfloat16 [2, 16, 1024, 1024], P(None, 'fsdp', 'seq'), may hold values from -6 to 6
- adapter_ids: int32 [2, 16], P(None, 'fsdp'), may hold values from 0 to 7
- in_weight: bfloat16 [1024, 3072], P('fsdp'), may hold values from -0.1875 to 0.1875
- out_weight: bfloat16 [1024, 1024], P('fsdp'), may hold values from -0.1875 to 0.1875
- gate_weight: bfloat16 [1024, 4608], P('fsdp'), may hold values from -0.1875 to 0.1875
- up_weight: bfloat16 [1024, 4608], P('fsdp'), may hold values from -0.1875 to 0.1875
- down_weight: bfloat16 [4608, 1024], P('fsdp'), may hold values from -0.09375 to 0.09375
- conv_weight: bfloat16 [3, 1024], replicated, may hold values from -3.5 to 3.5
- first_gain: bfloat16 [1024], replicated, may hold values from 0.099609375 to 1.8984375
- second_gain: bfloat16 [1024], replicated, may hold values from 0.099609375 to 1.8984375
- infirst_adapter: bfloat16 [1024, 128], replicated, may hold values from -0.1875 to 0.1875
- insecond_adapter: bfloat16 [128, 3072], replicated, may hold values from -1.5 to 1.5
- outfirst_adapter: bfloat16 [1024, 128], replicated, may hold values from -0.1875 to 0.1875
- outsecond_adapter: bfloat16 [128, 1024], replicated, may hold values from -1.5 to 1.5
- gatefirst_adapter: bfloat16 [1024, 128], replicated, may hold values from -0.1875 to 0.1875
- gatesecond_adapter: bfloat16 [128, 4608], replicated, may hold values from -1.5 to 1.5
- upfirst_adapter: bfloat16 [1024, 128], replicated, may hold values from -0.1875 to 0.1875
- upsecond_adapter: bfloat16 [128, 4608], replicated, may hold values from -1.5 to 1.5
- downfirst_adapter: bfloat16 [4608, 128], replicated, may hold values from -0.09375 to 0.09375
- downsecond_adapter: bfloat16 [128, 1024], replicated, may hold values from -1.5 to 1.5
Outputs:
- block_output: bfloat16 [2, 16, 1024, 1024], P(None, 'fsdp', 'seq')
- input_grad: bfloat16 [2, 16, 1024, 1024], P(None, 'fsdp', 'seq')
- infirst_grad: float32 [1024, 128], replicated
- insecond_grad: float32 [128, 3072], replicated
- outfirst_grad: float32 [1024, 128], replicated
- outsecond_grad: float32 [128, 1024], replicated
- gatefirst_grad: float32 [1024, 128], replicated
- gatesecond_grad: float32 [128, 4608], replicated
- upfirst_grad: float32 [1024, 128], replicated
- upsecond_grad: float32 [128, 4608], replicated
- downfirst_grad: float32 [4608, 128], replicated
- downsecond_grad: float32 [128, 1024], replicated
All inputs are finite; a program needn't handle non-finite values.
Results may differ from a plain program's by a relative error of at most 0.012.
The roundings to bfloat16 on the way count: a program that leaves them out, or rounds other values in their place, can miss the bound.
Values may be sent and summed in bfloat16 or wider, within the bound.
A program may use at most 256 MiB of HBM per device.

v0:
```python
import jax
import jax.numpy as jnp
from jax import lax
from jax.sharding import PartitionSpec as P

R = 16
EPSILON = 1e-05
ADAPTER_SCALE = 0.5


def from_behind(block, axis, distance):
    devices = range(lax.axis_size(axis))
    route = [(i - distance, i) for i in devices if i - distance in devices]
    return lax.ppermute(block, axis, route)


def forward_dot(left_side, right_side):
    return jnp.dot(left_side, right_side, preferred_element_type=jnp.float32)


def against_dot(left_side, right_side):
    return lax.dot_general(
        left_side, right_side, (((1,), (1,)), ((), ())), preferred_element_type=jnp.float32
    )


def outer_dot(left_side, right_side):
    return lax.dot_general(
        left_side, right_side, (((0,), (0,)), ((), ())), preferred_element_type=jnp.float32
    )


def adapted(inputs, weight, first_map, second_map, select):
    reduced = forward_dot(inputs, first_map).astype(jnp.bfloat16) * select
    result = forward_dot(inputs, weight) + ADAPTER_SCALE * forward_dot(reduced, second_map)
    return (result, reduced)


def adapted_back(grad_low, inputs, reduced, weight, first_map, second_map, select):
    grad_second = ADAPTER_SCALE * outer_dot(reduced, grad_low)
    grad_reduced = (ADAPTER_SCALE * against_dot(grad_low, second_map) * select).astype(jnp.bfloat16)
    grad_first = outer_dot(inputs, grad_reduced)
    grad_inputs = against_dot(grad_low, weight) + against_dot(grad_reduced, first_map)
    return (grad_inputs, grad_first, grad_second)


def rms_parts(values):
    inverse = lax.rsqrt(jnp.mean(values * values, axis=-1, keepdims=True) + EPSILON)
    return (inverse, values * inverse)


def rms_back(grad_normed, gain_vector, inverse, unit_rows):
    scaled = grad_normed * gain_vector
    return inverse * (scaled - unit_rows * jnp.mean(scaled * unit_rows, axis=-1, keepdims=True))


def per_device(
    block_input,
    output_grad,
    adapter_ids,
    in_weight,
    out_weight,
    gate_weight,
    up_weight,
    down_weight,
    conv_weight,
    first_gain,
    second_gain,
    infirst_adapter,
    insecond_adapter,
    outfirst_adapter,
    outsecond_adapter,
    gatefirst_adapter,
    gatesecond_adapter,
    upfirst_adapter,
    upsecond_adapter,
    downfirst_adapter,
    downsecond_adapter,
):
    batches, seq_count, local_len, features = block_input.shape
    row_count = seq_count * local_len
    adapters = (
        infirst_adapter,
        insecond_adapter,
        outfirst_adapter,
        outsecond_adapter,
        gatefirst_adapter,
        gatesecond_adapter,
        upfirst_adapter,
        upsecond_adapter,
        downfirst_adapter,
        downsecond_adapter,
    )
    slot_count = infirst_adapter.shape[1]
    kernel = conv_weight.astype(jnp.float32)
    gain_first = first_gain.astype(jnp.float32)
    gain_second = second_gain.astype(jnp.float32)
    owners = lax.broadcasted_iota(jnp.int32, (1, 1, slot_count), 2) // R
    totals = [jnp.zeros(member.shape, jnp.float32) for member in adapters]
    outputs = []
    input_grads = []
    for batch_index in range(batches):
        weight_in, weight_out, weight_gate, weight_up, weight_down = (
            lax.all_gather(in_weight, "fsdp", axis=0, tiled=True),
            lax.all_gather(out_weight, "fsdp", axis=0, tiled=True),
            lax.all_gather(gate_weight, "fsdp", axis=0, tiled=True),
            lax.all_gather(up_weight, "fsdp", axis=0, tiled=True),
            lax.all_gather(down_weight, "fsdp", axis=0, tiled=True),
        )
        inputs = block_input[batch_index].reshape(row_count, features).astype(jnp.float32)
        matches = owners == adapter_ids[batch_index][:, None, None]
        select = (
            jnp.broadcast_to(matches, (seq_count, local_len, slot_count))
            .reshape(row_count, slot_count)
            .astype(jnp.bfloat16)
        )
        inverse_first, unit_first = rms_parts(inputs)
        normed = (unit_first * gain_first).astype(jnp.bfloat16)
        mixed_in, low_in = adapted(normed, weight_in, adapters[0], adapters[1], select)
        first_part = mixed_in[:, :features]
        middle_part = mixed_in[:, features : 2 * features]
        last_part = mixed_in[:, 2 * features :]
        gated_values = (first_part * last_part).reshape(seq_count, local_len, features)
        rim_rows = from_behind(gated_values[:, local_len - 2 :, :], "seq", 1)
        extended = jnp.concatenate([rim_rows, gated_values], axis=1)
        conv_out = (
            kernel[0] * extended[:, :local_len]
            + kernel[1] * extended[:, 1 : local_len + 1]
            + kernel[2] * extended[:, 2:]
        ).reshape(row_count, features)
        mixer_out = (middle_part * conv_out).astype(jnp.bfloat16)
        branch, low_out = adapted(mixer_out, weight_out, adapters[2], adapters[3], select)
        after_mixer = inputs + branch
        inverse_second, unit_second = rms_parts(after_mixer)
        second = (unit_second * gain_second).astype(jnp.bfloat16)
        gate_value, low_gate = adapted(second, weight_gate, adapters[4], adapters[5], select)
        up_value, low_up = adapted(second, weight_up, adapters[6], adapters[7], select)
        sigmoid_gate = jax.nn.sigmoid(gate_value)
        activated = gate_value * sigmoid_gate
        hidden = (activated * up_value).astype(jnp.bfloat16)
        down_value, low_down = adapted(hidden, weight_down, adapters[8], adapters[9], select)
        outputs.append(
            (after_mixer + down_value).astype(jnp.bfloat16).reshape(seq_count, local_len, features)
        )
        weight_in, weight_out, weight_gate, weight_up, weight_down = (
            lax.all_gather(in_weight, "fsdp", axis=0, tiled=True),
            lax.all_gather(out_weight, "fsdp", axis=0, tiled=True),
            lax.all_gather(gate_weight, "fsdp", axis=0, tiled=True),
            lax.all_gather(up_weight, "fsdp", axis=0, tiled=True),
            lax.all_gather(down_weight, "fsdp", axis=0, tiled=True),
        )
        cotangent = output_grad[batch_index].reshape(row_count, features)
        grad_hidden, grad_first, grad_second = adapted_back(
            cotangent, hidden, low_down, weight_down, adapters[8], adapters[9], select
        )
        totals[8] = totals[8] + grad_first
        totals[9] = totals[9] + grad_second
        grad_gate = (
            grad_hidden * up_value * sigmoid_gate * (1.0 + gate_value * (1.0 - sigmoid_gate))
        ).astype(jnp.bfloat16)
        grad_upper = (grad_hidden * activated).astype(jnp.bfloat16)
        back_gate, grad_first, grad_second = adapted_back(
            grad_gate, second, low_gate, weight_gate, adapters[4], adapters[5], select
        )
        totals[4] = totals[4] + grad_first
        totals[5] = totals[5] + grad_second
        back_upper, grad_first, grad_second = adapted_back(
            grad_upper, second, low_up, weight_up, adapters[6], adapters[7], select
        )
        totals[6] = totals[6] + grad_first
        totals[7] = totals[7] + grad_second
        grad_after = cotangent.astype(jnp.float32) + rms_back(
            back_gate + back_upper, gain_second, inverse_second, unit_second
        )
        grad_mixer, grad_first, grad_second = adapted_back(
            grad_after.astype(jnp.bfloat16),
            mixer_out,
            low_out,
            weight_out,
            adapters[2],
            adapters[3],
            select,
        )
        totals[2] = totals[2] + grad_first
        totals[3] = totals[3] + grad_second
        grad_conv = (grad_mixer * middle_part).reshape(seq_count, local_len, features)
        rim_back = from_behind(grad_conv[:, :2, :], "seq", -1)
        beyond = jnp.concatenate([grad_conv, rim_back], axis=1)
        grad_gated = (
            kernel[2] * beyond[:, :local_len]
            + kernel[1] * beyond[:, 1 : local_len + 1]
            + kernel[0] * beyond[:, 2:]
        ).reshape(row_count, features)
        grad_mixed = jnp.concatenate(
            [grad_gated * last_part, grad_mixer * conv_out, grad_gated * first_part], axis=1
        ).astype(jnp.bfloat16)
        grad_normed, grad_first, grad_second = adapted_back(
            grad_mixed, normed, low_in, weight_in, adapters[0], adapters[1], select
        )
        totals[0] = totals[0] + grad_first
        totals[1] = totals[1] + grad_second
        grad_input = grad_after + rms_back(grad_normed, gain_first, inverse_first, unit_first)
        input_grads.append(grad_input.astype(jnp.bfloat16).reshape(seq_count, local_len, features))
    summed = lax.psum(
        (
            totals[0],
            totals[1],
            totals[2],
            totals[3],
            totals[4],
            totals[5],
            totals[6],
            totals[7],
            totals[8],
            totals[9],
        ),
        ("fsdp", "seq"),
    )
    return (
        jnp.stack(outputs),
        jnp.stack(input_grads),
        summed[0],
        summed[1],
        summed[2],
        summed[3],
        summed[4],
        summed[5],
        summed[6],
        summed[7],
        summed[8],
        summed[9],
    )


def solution(mesh):
    return jax.shard_map(
        per_device,
        mesh=mesh,
        in_specs=(
            P(None, "fsdp", "seq", None),
            P(None, "fsdp", "seq", None),
            P(None, "fsdp"),
            P("fsdp", None),
            P("fsdp", None),
            P("fsdp", None),
            P("fsdp", None),
            P("fsdp", None),
            P(),
            P(),
            P(),
            P(),
            P(),
            P(),
            P(),
            P(),
            P(),
            P(),
            P(),
            P(),
            P(),
        ),
        out_specs=(
            P(None, "fsdp", "seq", None),
            P(None, "fsdp", "seq", None),
            P(),
            P(),
            P(),
            P(),
            P(),
            P(),
            P(),
            P(),
            P(),
            P(),
        ),
        check_vma=False,
    )
```

profile of v0, /device:TPU:0, one launch (start us, length us, event | category | flops | bytes accessed | tf_op | source)
XLA Modules:
  0.0 815.4 jit_solution(7204211921925107187)
XLA Ops:
  14.0 2.0 fusion.43
  19.3 55.6 %all-gather.6.cloned.1.call-done = bf16[1024,3072]{1,0:T(8,128)(2,1)} async-done(((bf16[64,3072]{1,0:T(8,128)(2,1)}), bf16[1024,3072]{1,0:T(8,128)(2,1)}) %all-gather.6.cloned.1.call-update) | async-done | bytes 6291472 | tf_op jit(solution)/shard_map/all_gather | solution.py:104
  74.9 5.9 fusion.106
  82.4 3.4 collective-permute-start.1
  85.8 3.6 fusion.111
  91.0 1.5 collective-permute-start
  93.7 3.7 multiply_convert_fusion.15
  98.8 1.7 fusion.119
  100.5 1.7 fusion.123
  102.3 14.8 %all-gather.8.cloned.1.call-done = bf16[1024,1024]{1,0:T(8,128)(2,1)} async-done(((bf16[64,1024]{1,0:T(8,128)(2,1)}), bf16[1024,1024]{1,0:T(8,128)(2,1)}) %all-gather.8.cloned.1.call-update) | async-done | bytes 2097168 | tf_op jit(solution)/shard_map/all_gather | solution.py:105
  117.1 4.2 multiply_reduce_fusion.3
  121.3 1.5 multiply_reduce_fusion.2
  127.3 72.4 %all-gather.12.cloned.1.call-done = bf16[1024,4608]{1,0:T(8,128)(2,1)} async-done(((bf16[64,4608]{1,0:T(8,128)(2,1)}), bf16[1024,4608]{1,0:T(8,128)(2,1)}) %all-gather.12.cloned.1.call-update) | async-done | bytes 9437200 | tf_op jit(solution)/shard_map/all_gather | solution.py:107
  199.6 7.7 fusion.121
  207.3 4.9 multiply_add_fusion.2
  212.2 69.2 %all-gather.14.cloned.1.call-done = bf16[4608,1024]{1,0:T(8,128)(2,1)} async-done(((bf16[288,1024]{1,0:T(8,128)(2,1)}), bf16[4608,1024]{1,0:T(8,128)(2,1)}) %all-gather.14.cloned.1.call-update) | async-done | bytes 9437200 | tf_op jit(solution)/shard_map/all_gather | solution.py:108
  281.4 8.3 %fusion.82 = f32[512,4608]{1,0:T(8,128)S(1)} fusion(bf16[4608,1024]{1,0:T(8,128)(2,1)} %all-gather.14.cloned.1.call-done, bf16[2,1,512,1024]{3,2,1,0:T(8,128)(2,1)} %param.22), kind=kOutput, calls=%fused_computation.178 | convolution fusion | flops 4831838208 | bytes 19922944 | tf_op jit(solution)/shard_map/dot_general | solution.py:22
  289.7 5.0 convolution_add_fusion.1
  294.7 68.5 %all-gather.10.cloned.1.call-done = bf16[1024,4608]{1,0:T(8,128)(2,1)} async-done(((bf16[64,4608]{1,0:T(8,128)(2,1)}), bf16[1024,4608]{1,0:T(8,128)(2,1)}) %all-gather.10.cloned.1.call-update) | async-done | bytes 9437200 | tf_op jit(solution)/shard_map/all_gather | solution.py:106
  363.1 11.0 %fusion.120 = f32[512,4608]{1,0:T(8,128)} fusion(bf16[512,1024]{1,0:T(8,128)(2,1)S(1)} %get-tuple-element.55, bf16[1024,4608]{1,0:T(8,128)(2,1)} %all-gather.10.cloned.1.call-done), kind=kOutput, calls=%fused_computation.222 | convolution fusion | flops 4831838208 | bytes 19922944 | tf_op jit(solution)/shard_map/dot_general | solution.py:18
  374.2 16.5 %multiply_convert_fusion.3 = (bf16[512,4608]{1,0:T(8,128)(2,1)}, bf16[512,4608]{1,0:T(8,128)(2,1)}, bf16[512,4608]{1,0:T(8,128)(2,1)S(1)}) fusion(f32[512,4608]{1,0:T(8,128)} %convolution_add_fusion.1, f32[512,4608]{1,0:T(8,128)} %multiply_add_fusion.2, f32[512,4608]{1,0:T(8,128)} %fusion.120, bf16[512,128]{1,0:T(8,128)(2,1)} %fusion.67, ...), kind=kOutput, calls=%fused_computation.3 | convolution fusion | flops 644087808 | bytes 43778048 | tf_op jit(solution)/shard_map/dot_general | solution.py:18
  390.7 2.2 copy-done.28
  392.9 3.5 fusion.63
  396.4 3.9 fusion.140
  400.3 2.2 fusion.139
  402.6 1.4 fusion.58
  404.0 2.2 fusion.137
  406.2 1.4 fusion.57
  408.9 1.7 fusion.128
  411.9 7.6 fusion.125
  419.5 4.9 multiply_add_fusion
  424.4 7.9 fusion.77
  432.3 5.0 convolution_add_fusion
  437.3 11.0 %fusion.124 = f32[512,4608]{1,0:T(8,128)} fusion(bf16[512,1024]{1,0:T(8,128)(2,1)S(1)} %get-tuple-element.56, bf16[1024,4608]{1,0:T(8,128)(2,1)} %all-gather.10.cloned.1.call-done), kind=kOutput, calls=%fused_computation.226 | convolution fusion | flops 4831838208 | bytes 19922944 | tf_op jit(solution)/shard_map/dot_general | solution.py:18
  448.4 16.3 %multiply_convert_fusion.1 = (bf16[512,4608]{1,0:T(8,128)(2,1)S(1)}, bf16[512,4608]{1,0:T(8,128)(2,1)}, bf16[512,4608]{1,0:T(8,128)(2,1)}) fusion(f32[512,4608]{1,0:T(8,128)} %convolution_add_fusion, f32[512,4608]{1,0:T(8,128)} %multiply_add_fusion, f32[512,4608]{1,0:T(8,128)} %fusion.124, bf16[512,128]{1,0:T(8,128)(2,1)} %fusion.71, ...), kind=kOutput, calls=%fused_computation.1 | convolution fusion | flops 644087808 | bytes 43778048 | tf_op jit(solution)/shard_map/dot_general | solution.py:18
  464.6 5.8 fusion.61
  470.4 1.4 fusion.60
  472.3 7.9 fusion.131
  480.2 7.8 fusion.133
  489.1 7.9 fusion.127
  497.0 8.0 fusion.129
  510.7 1.4 fusion.64
  512.1 2.9 convolution_add_fusion.2
  515.0 2.2 fusion.3
  518.6 2.3 fusion.2
  528.0 1.9 multiply_convert_fusion.7
  529.9 1.8 collective-permute-start.3
  535.9 1.7 multiply_convert_fusion.10
  540.0 3.1 collective-permute-done.2
  543.2 3.9 multiply_convert_fusion.11
  553.8 1.8 fusion.4
  556.3 1.4 convolution_add_fusion.13
  557.8 9.9 %fusion.122 = f32[512,1024]{1,0:T(8,128)S(1)} fusion(bf16[512,4608]{1,0:T(8,128)(2,1)} %copy-done.28, bf16[4608,1024]{1,0:T(8,128)(2,1)} %all-gather.14.cloned.1.call-done), kind=kOutput, calls=%fused_computation.224 | convolution fusion | flops 4831838208 | bytes 16252928 | tf_op jit(solution)/shard_map/dot_general | solution.py:18
  568.2 9.6 %fusion.126 = f32[512,1024]{1,0:T(8,128)S(1)} fusion(bf16[512,4608]{1,0:T(8,128)(2,1)} %get-tuple-element.39, bf16[4608,1024]{1,0:T(8,128)(2,1)} %all-gather.14.cloned.1.call-done), kind=kOutput, calls=%fused_computation.228 | convolution fusion | flops 4831838208 | bytes 16252928 | tf_op jit(solution)/shard_map/dot_general | solution.py:18
  578.2 1.5 pad_maximum_fusion.6
  581.6 3.5 add_multiply_fusion
  585.2 6.9 fusion.38
  593.2 1.5 pad_maximum_fusion.7
  594.7 198.8 %all-reduce.3.cloned.1.call-done = (f32[1024,128]{1,0:T(8,128)}, f32[128,3072]{1,0:T(8,128)}, f32[1024,128]{1,0:T(8,128)}, f32[128,1024]{1,0:T(8,128)}, f32[1024...) async-done(((f32[1024,128]{1,0:T(8,128)}, f32[128,3072]{1,0:T(8,128)}, ...) | async-done | bytes 11796496 | tf_op jit(solution)/shard_map/psum | solution.py:204
  793.6 1.9 copy.43
  795.5 2.8 copy.44
  800.7 1.4 copy.48
  803.6 1.4 copy.50
  806.1 1.4 copy.51
  (398 shorter events, 61.3 us)
Async XLA Ops:
  7.2 367.0 %copy-start = (bf16[128,4608]{1,0:T(8,128)(2,1)S(1)}, bf16[128,4608]{1,0:T(8,128)(2,1)}, u32[]{:S(2)}) copy-start(bf16[128,4608]{1,0:T(8,128)(2,1)} %param.37) | copy-start | bytes 3538948
  7.2 67.7 %all-gather.6.cloned.1.call-start = ((), (), s32[]{:S(2)}) async-start(), calls=%async_computation | async-start | bytes 6684672 | tf_op jit(solution)/shard_map/all_gather | solution.py:104
  7.9 8.1 copy-start.18
  8.0 8.1 copy-start.70
  8.0 109.1 %all-gather.8.cloned.1.call-start = ((), (), s32[]{:S(2)}) async-start(), calls=%async_computation.1 | async-start | bytes 2228224 | tf_op jit(solution)/shard_map/all_gather | solution.py:105
  8.7 190.9 %all-gather.12.cloned.1.call-start = ((), (), s32[]{:S(2)}) async-start(), calls=%async_computation.3 | async-start | bytes 10027008 | tf_op jit(solution)/shard_map/all_gather | solution.py:107
  9.5 271.9 %all-gather.14.cloned.1.call-start = ((), (), s32[]{:S(2)}) async-start(), calls=%async_computation.4 | async-start | bytes 10027008 | tf_op jit(solution)/shard_map/all_gather | solution.py:108
  10.0 353.1 %all-gather.10.cloned.1.call-start = ((), (), s32[]{:S(2)}) async-start(), calls=%async_computation.2 | async-start | bytes 10027008 | tf_op jit(solution)/shard_map/all_gather | solution.py:106
  10.6 783.0 %all-reduce.3.cloned.1.call-start = ((), (), s32[]{:S(2)}) async-start(), calls=%async_computation.5 | async-start | bytes 23592960 | tf_op jit(solution)/shard_map/psum | solution.py:204
  10.7 75.1 %copy-start.115 = (f32[1024]{0:T(1024)}, f32[1024]{0:T(1024)S(1)}, u32[]{:S(2)}) copy-start(f32[1024]{0:T(1024)S(1)} %convert_element_type.169) | copy-start | bytes 12292
  11.9 6.8 copy-start.127
  16.0 58.9 %copy-start.111 = (f32[512]{0:T(512)}, f32[512]{0:T(512)S(1)}, u32[]{:S(2)}) copy-start(f32[512]{0:T(512)S(1)} %add_rsqrt_fusion.1) | copy-start | bytes 6148
  16.1 69.7 %copy-start.113 = (f32[512]{0:T(512)}, f32[512]{0:T(512)S(1)}, u32[]{:S(2)}) copy-start(f32[512]{0:T(512)S(1)} %add_rsqrt_fusion.3) | copy-start | bytes 6148
  18.8 62.0 %copy-start.91 = (bf16[512,128]{1,0:T(8,128)(2,1)}, bf16[512,128]{1,0:T(8,128)(2,1)S(1)}, u32[]{:S(2)}) copy-start(bf16[512,128]{1,0:T(8,128)(2,1)S(1)} %fusion.69) | copy-start | bytes 393220
  18.8 56.1 %copy-start.24 = (bf16[2,1,512,1024]{3,2,1,0:T(8,128)(2,1)S(1)}, bf16[2,1,512,1024]{3,2,1,0:T(8,128)(2,1)}, u32[]{:S(2)}) copy-start(bf16[2,1,512,1024]{3,2,1,0:T(8,128)(2,1)} %param.21) | copy-start | bytes 6291460
  19.3 70.1 %copy-start.93 = (bf16[512,128]{1,0:T(8,128)(2,1)}, bf16[512,128]{1,0:T(8,128)(2,1)S(1)}, u32[]{:S(2)}) copy-start(bf16[512,128]{1,0:T(8,128)(2,1)S(1)} %fusion.65) | copy-start | bytes 393220
  74.9 5.9 copy-start.41
  74.9 10.9 %slice-start.18 = ((s8[6291456]{0:T(1024)(128)(4,1)}), s8[4194304]{0:T(1024)(128)(4,1)S(1)}, s32[]{:S(2)}) async-start(s8[6291456]{0:T(1024)(128)(4,1)} %bitcast.241), calls=%async_computation.24 | async-start | bytes 8388608
  80.8 5.0 slice-start.19
  81.8 11.9 %copy-start.2 = (f32[512,3072]{1,0:T(8,128)}, f32[512,3072]{1,0:T(8,128)S(1)}, u32[]{:S(2)}) copy-start(f32[512,3072]{1,0:T(8,128)S(1)} %multiply_add_fusion.4) | copy-start | bytes 18874372
  82.4 10.2 %collective-permute-start.1 = (f32[1,2,1024]{2,1,0:T(2,128)S(1)}, f32[1,2,1024]{2,1,0:T(2,128)S(1)}, u32[]{:S(2)}, u32[]{:S(2)}) collective-permute-start(f32[1,2,1024]{2,1,0:T(2,128)S(1)} %slice.129), channel_id=1, source_target_pairs={{0,1},{2,3},{4,5},{6,7},{8,9},{10,11},{12,13},{14,15},{16,17},{18,... | collective-permute-start | bytes 24584 | tf_op jit(solution)/shard_map/ppermute | solution.py:14
  91.0 2.7 collective-permute-start
  92.6 30.3 %copy-start.98 = (f32[1024]{0:T(1024)}, f32[1024]{0:T(1024)S(1)}, u32[]{:S(2)}) copy-start(f32[1024]{0:T(1024)S(1)} %convert_element_type.175) | copy-start | bytes 12292
  124.2 313.2 %copy-start.16 = (bf16[512,1024]{1,0:T(8,128)(2,1)}, bf16[512,1024]{1,0:T(8,128)(2,1)S(1)}, u32[]{:S(2)}) copy-start(bf16[512,1024]{1,0:T(8,128)(2,1)S(1)} %get-tuple-element.56) | copy-start | bytes 3145732
  126.2 293.3 %copy-start.49 = (bf16[512,128]{1,0:T(8,128)(2,1)}, bf16[512,128]{1,0:T(8,128)(2,1)S(1)}, u32[]{:S(2)}) copy-start(bf16[512,128]{1,0:T(8,128)(2,1)S(1)} %fusion.72) | copy-start | bytes 393220
  199.6 7.7 copy-start.29
  281.4 8.3 %copy-start.31 = (bf16[4608,128]{1,0:T(8,128)(2,1)S(1)}, bf16[4608,128]{1,0:T(8,128)(2,1)}, u32[]{:S(2)}) copy-start(bf16[4608,128]{1,0:T(8,128)(2,1)} %param.40) | copy-start | bytes 3538948
  281.4 8.3 %copy-start.76 = (bf16[512,128]{1,0:T(8,128)(2,1)S(1)}, bf16[512,128]{1,0:T(8,128)(2,1)}, u32[]{:S(2)}) copy-start(bf16[512,128]{1,0:T(8,128)(2,1)} %fusion.53) | copy-start | bytes 393220
  392.9 7.4 slice-start.10
  396.4 7.6 slice-start.14
  404.0 6.7 copy-start.78
  424.4 8.0 copy-start.32
  424.4 8.0 copy-start.74
  448.4 16.3 %copy-start.121 = (f32[128]{0:T(128)S(1)}, f32[128]{0:T(128)}, u32[]{:S(2)}) copy-start(f32[128]{0:T(128)} %copy-done.120) | copy-start | bytes 1540
  464.6 7.6 copy-start.13
  471.8 8.3 %slice-start.6 = ((s8[4718592]{0:T(1024)(128)(4,1)}), s8[4194304]{0:T(1024)(128)(4,1)S(1)}, s32[]{:S(2)}) async-start(s8[4718592]{0:T(1024)(128)(4,1)} %bitcast.223), calls=%async_computation.12 | async-start | bytes 8388608
  472.3 7.9 slice-start.7
  472.3 16.8 %slice-start.16 = ((s8[4718592]{0:T(1024)(128)(4,1)}), s8[4194304]{0:T(1024)(128)(4,1)S(1)}, s32[]{:S(2)}) async-start(s8[4718592]{0:T(1024)(128)(4,1)} %bitcast.233), calls=%async_computation.22 | async-start | bytes 8388608
  480.2 7.8 copy-start.5
  480.2 7.8 copy-start.67
  480.2 7.8 copy-start.99
  480.2 7.8 copy-start.107
  480.2 8.8 %slice-start.17 = ((s8[4718592]{0:T(1024)(128)(4,1)}), s8[524288]{0:T(1024)(128)(4,1)S(1)}, s32[]{:S(2)}) async-start(s8[4718592]{0:T(1024)(128)(4,1)} %bitcast.233), calls=%async_computation.23 | async-start | bytes 1048576
  488.1 8.9 %slice-start.12 = ((s8[4718592]{0:T(1024)(128)(4,1)}), s8[4194304]{0:T(1024)(128)(4,1)S(1)}, s32[]{:S(2)}) async-start(s8[4718592]{0:T(1024)(128)(4,1)} %bitcast.229), calls=%async_computation.18 | async-start | bytes 8388608
  489.1 7.9 slice-start.13
  497.0 8.0 copy-start.7
  497.0 8.0 copy-start.27
  497.0 8.0 copy-start.79
  497.0 8.0 copy-start.109
  507.8 16.9 %copy-start.11 = (f32[512,1024]{1,0:T(8,128)}, f32[512,1024]{1,0:T(8,128)S(1)}, u32[]{:S(2)}) copy-start(f32[512,1024]{1,0:T(8,128)S(1)} %get-tuple-element.45) | copy-start | bytes 6291460
  507.8 25.2 %copy-start.9 = (f32[512,1024]{1,0:T(8,128)}, f32[512,1024]{1,0:T(8,128)S(1)}, u32[]{:S(2)}) copy-start(f32[512,1024]{1,0:T(8,128)S(1)} %get-tuple-element.44) | copy-start | bytes 6291460
  512.1 6.5 slice-start.4
  528.0 6.8 slice-start.2
  529.9 10.2 %collective-permute-start.3 = (f32[1,2,1024]{2,1,0:T(2,128)S(1)}, f32[1,2,1024]{2,1,0:T(2,128)S(1)}, u32[]{:S(2)}, u32[]{:S(2)}) collective-permute-start(f32[1,2,1024]{2,1,0:T(2,128)S(1)} %slice.135), channel_id=1, source_target_pairs={{1,0},{3,2},{5,4},{7,6},{9,8},{11,10},{13,12},{15,14},{17,16},{19,... | collective-permute-start | bytes 24584 | tf_op jit(solution)/shard_map/ppermute | solution.py:14
  537.6 5.6 copy-start.101
  537.6 5.6 copy-start.103
  537.6 5.6 copy-start.105
  537.6 5.5 collective-permute-start.2
  557.7 10.0 %copy-start.8 = (f32[512,1024]{1,0:T(8,128)S(1)}, f32[512,1024]{1,0:T(8,128)}, u32[]{:S(2)}) copy-start(f32[512,1024]{1,0:T(8,128)} %copy-done.6) | copy-start | bytes 6291460
  557.8 10.0 %copy-start.71 = (bf16[128,1024]{1,0:T(8,128)(2,1)S(1)}, bf16[128,1024]{1,0:T(8,128)(2,1)}, u32[]{:S(2)}) copy-start(bf16[128,1024]{1,0:T(8,128)(2,1)} %param.41) | copy-start | bytes 786436
  567.7 12.9 %slice-start.20 = ((s8[6291456]{0:T(1024)(128)(4,1)}), s8[4194304]{0:T(1024)(128)(4,1)S(1)}, s32[]{:S(2)}) async-start(s8[6291456]{0:T(1024)(128)(4,1)} %bitcast.243), calls=%async_computation.26 | async-start | bytes 8388608
  568.2 12.5 %slice-start.21 = ((s8[6291456]{0:T(1024)(128)(4,1)}), s8[2097152]{0:T(1024)(128)(4,1)S(1)}, s32[]{:S(2)}) async-start(s8[6291456]{0:T(1024)(128)(4,1)} %bitcast.243), calls=%async_computation.27 | async-start | bytes 4194304
  585.2 6.9 copy-start.10
  585.2 6.9 copy-start.12
  (97 other events, 237.9 us)
Sparse Core Ops, SparseCore 0:
  10.3 64.5 all-gather.5
  77.1 39.9 all-gather.7
  119.4 80.2 all-gather.11
  201.8 79.5 all-gather.13
  283.5 79.5 all-gather.9
  557.9 235.6 all-reduce.2
where the time goes:
time: 823 us; the launch traced here: 815 us
  waiting for transfers between devices  487 us (59%)
  matrix products  252 us (31%)
  local copies, waits for them, and re-layouts  28.7 us (3%)
  other arithmetic  23.6 us (3%)
  between operations  16.2 us (2%)
    psum x1, waiting for transfers between devices, per_device(): lax.psum((totals[0], totals[1], totals[2], totals[3], totals[4], totals[5...  199 us
    dot_general x30, matrix products, forward_dot(): return jnp.dot(left_side, right_side, preferred_element_type=jnp.float32)  131 us
    dot_general x30, matrix products, against_dot(): lax.dot_general(left_side, right_side, (((1,), (1,)), ((), ())), preferre...  91.5 us
    all_gather x1, waiting for transfers between devices, per_device(): lax.all_gather(up_weight, 'fsdp', axis=0, tiled=True)  72.4 us
    all_gather x1, waiting for transfers between devices, per_device(): lax.all_gather(down_weight, 'fsdp', axis=0, tiled=True)  69.2 us
    all_gather x1, waiting for transfers between devices, per_device(): lax.all_gather(gate_weight, 'fsdp', axis=0, tiled=True)  68.5 us
    all_gather x1, waiting for transfers between devices, per_device(): lax.all_gather(in_weight, 'fsdp', axis=0, tiled=True)  55.6 us
    dot_general x20, matrix products, outer_dot(): lax.dot_general(left_side, right_side, (((0,), (0,)), ((), ())), preferre...  30 us
  transfers between devices with their start and end apart: 10, of which 8 were waited for; matrix products, arithmetic and copies ran while one was open for 13% of the time, Pallas kernels for 0%

commit v1 on v0

--- a/solution.py
+++ b/solution.py
@@ -201,7 +201,7 @@
         totals[1] = totals[1] + grad_second
         grad_input = grad_after + rms_back(grad_normed, gain_first, inverse_first, unit_first)
         input_grads.append(grad_input.astype(jnp.bfloat16).reshape(seq_count, local_len, features))
-    summed = lax.psum(
+    half = lax.psum(
         (
             totals[0],
             totals[1],
@@ -214,8 +214,9 @@
             totals[8],
             totals[9],
         ),
-        ("fsdp", "seq"),
-    )
+        "seq",
+    )
+    summed = lax.psum(half, "fsdp")
     return (
         jnp.stack(outputs),
         jnp.stack(input_grads),

time: 823 us -> 1090 us (1.32)
  waiting for transfers between devices: 487 us -> 753 us
    psum x0 -> x1, waiting for transfers between devices: none -> 192 us  [per_device(): summed = lax.psum(half, 'fsdp')]
    psum x1, waiting for transfers between devices: 199 us -> 273 us  [per_device(): lax.psum((totals[0], totals[1], totals[2], totals[3], totals[4], totals[5...]
  transfers between devices with their start and end apart: 10 -> 11, of which waited for: 8 -> 9; matrix products, arithmetic and copies ran while one was open for 13% -> 10% of each run, Pallas kernels for 0% -> 0%
where the time goes in v1:
time: 1090 us; the launch traced here: 1080 us
  waiting for transfers between devices  753 us (69%)
  matrix products  252 us (23%)
  local copies, waits for them, and re-layouts  28.8 us (3%)
  other arithmetic  23.5 us (2%)
  between operations  16.3 us (1%)
    psum x1, waiting for transfers between devices, per_device(): lax.psum((totals[0], totals[1], totals[2], totals[3], totals[4], totals[5...  273 us
    psum x1, waiting for transfers between devices, per_device(): summed = lax.psum(half, 'fsdp')  192 us
    dot_general x30, matrix products, forward_dot(): return jnp.dot(left_side, right_side, preferred_element_type=jnp.float32)  131 us
    dot_general x30, matrix products, against_dot(): lax.dot_general(left_side, right_side, (((1,), (1,)), ((), ())), preferre...  91.4 us
    all_gather x1, waiting for transfers between devices, per_device(): lax.all_gather(up_weight, 'fsdp', axis=0, tiled=True)  72.4 us
    all_gather x1, waiting for transfers between devices, per_device(): lax.all_gather(down_weight, 'fsdp', axis=0, tiled=True)  69.1 us
    all_gather x1, waiting for transfers between devices, per_device(): lax.all_gather(gate_weight, 'fsdp', axis=0, tiled=True)  68.5 us
    all_gather x1, waiting for transfers between devices, per_device(): lax.all_gather(in_weight, 'fsdp', axis=0, tiled=True)  55.6 us
  transfers between devices with their start and end apart: 11, of which 9 were waited for; matrix products, arithmetic and copies ran while one was open for 10% of the time, Pallas kernels for 0%

profile of v1, /device:TPU:0, one launch (start us, length us, event | category | flops | bytes accessed | tf_op | source)
XLA Modules:
  0.0 1082.4 jit_solution(7550105549889263009)
XLA Ops:
  14.0 2.0 fusion.43
  19.3 55.6 %all-gather.6.cloned.1.call-done = bf16[1024,3072]{1,0:T(8,128)(2,1)} async-done(((bf16[64,3072]{1,0:T(8,128)(2,1)}), bf16[1024,3072]{1,0:T(8,128)(2,1)}) %all-gather.6.cloned.1.call-update) | async-done | bytes 6291472 | tf_op jit(solution)/shard_map/all_gather | solution.py:104
  74.9 5.9 fusion.106
  82.4 3.4 collective-permute-start.1
  85.8 3.6 fusion.111
  91.0 1.5 collective-permute-start
  93.7 3.7 multiply_convert_fusion.15
  98.8 1.7 fusion.119
  100.5 1.7 fusion.123
  102.3 14.8 %all-gather.8.cloned.1.call-done = bf16[1024,1024]{1,0:T(8,128)(2,1)} async-done(((bf16[64,1024]{1,0:T(8,128)(2,1)}), bf16[1024,1024]{1,0:T(8,128)(2,1)}) %all-gather.8.cloned.1.call-update) | async-done | bytes 2097168 | tf_op jit(solution)/shard_map/all_gather | solution.py:105
  117.1 4.2 multiply_reduce_fusion.3
  121.3 1.5 multiply_reduce_fusion.2
  127.3 72.4 %all-gather.12.cloned.1.call-done = bf16[1024,4608]{1,0:T(8,128)(2,1)} async-done(((bf16[64,4608]{1,0:T(8,128)(2,1)}), bf16[1024,4608]{1,0:T(8,128)(2,1)}) %all-gather.12.cloned.1.call-update) | async-done | bytes 9437200 | tf_op jit(solution)/shard_map/all_gather | solution.py:107
  199.6 7.7 fusion.121
  207.3 4.9 multiply_add_fusion.2
  212.2 69.1 %all-gather.14.cloned.1.call-done = bf16[4608,1024]{1,0:T(8,128)(2,1)} async-done(((bf16[288,1024]{1,0:T(8,128)(2,1)}), bf16[4608,1024]{1,0:T(8,128)(2,1)}) %all-gather.14.cloned.1.call-update) | async-done | bytes 9437200 | tf_op jit(solution)/shard_map/all_gather | solution.py:108
  281.4 8.3 fusion.82
  289.7 5.0 convolution_add_fusion.1
  294.6 68.5 %all-gather.10.cloned.1.call-done = bf16[1024,4608]{1,0:T(8,128)(2,1)} async-done(((bf16[64,4608]{1,0:T(8,128)(2,1)}), bf16[1024,4608]{1,0:T(8,128)(2,1)}) %all-gather.10.cloned.1.call-update) | async-done | bytes 9437200 | tf_op jit(solution)/shard_map/all_gather | solution.py:106
  363.1 11.0 %fusion.120 = f32[512,4608]{1,0:T(8,128)} fusion(bf16[512,1024]{1,0:T(8,128)(2,1)S(1)} %get-tuple-element.65, bf16[1024,4608]{1,0:T(8,128)(2,1)} %all-gather.10.cloned.1.call-done), kind=kOutput, calls=%fused_computation.222 | convolution fusion | flops 4831838208 | bytes 19922944 | tf_op jit(solution)/shard_map/dot_general | solution.py:18
  374.2 16.4 %multiply_convert_fusion.3 = (bf16[512,4608]{1,0:T(8,128)(2,1)}, bf16[512,4608]{1,0:T(8,128)(2,1)}, bf16[512,4608]{1,0:T(8,128)(2,1)S(1)}) fusion(f32[512,4608]{1,0:T(8,128)} %convolution_add_fusion.1, f32[512,4608]{1,0:T(8,128)} %multiply_add_fusion.2, f32[512,4608]{1,0:T(8,128)} %fusion.120, bf16[512,128]{1,0:T(8,128)(2,1)} %fusion.67, ...), kind=kOutput, calls=%fused_computation.3 | convolution fusion | flops 644087808 | bytes 43778048 | tf_op jit(solution)/shard_map/dot_general | solution.py:18
  390.6 2.2 copy-done.28
  392.8 3.5 fusion.63
  396.3 3.9 fusion.140
  400.3 2.2 fusion.139
  402.5 1.4 fusion.58
  403.9 2.2 fusion.137
  408.8 1.7 fusion.128
  411.8 7.6 fusion.125
  419.4 4.9 multiply_add_fusion
  424.3 7.9 fusion.77
  432.3 5.0 convolution_add_fusion
  437.3 11.0 %fusion.124 = f32[512,4608]{1,0:T(8,128)} fusion(bf16[512,1024]{1,0:T(8,128)(2,1)S(1)} %get-tuple-element.66, bf16[1024,4608]{1,0:T(8,128)(2,1)} %all-gather.10.cloned.1.call-done), kind=kOutput, calls=%fused_computation.226 | convolution fusion | flops 4831838208 | bytes 19922944 | tf_op jit(solution)/shard_map/dot_general | solution.py:18
  448.3 16.2 %multiply_convert_fusion.1 = (bf16[512,4608]{1,0:T(8,128)(2,1)S(1)}, bf16[512,4608]{1,0:T(8,128)(2,1)}, bf16[512,4608]{1,0:T(8,128)(2,1)}) fusion(f32[512,4608]{1,0:T(8,128)} %convolution_add_fusion, f32[512,4608]{1,0:T(8,128)} %multiply_add_fusion, f32[512,4608]{1,0:T(8,128)} %fusion.124, bf16[512,128]{1,0:T(8,128)(2,1)} %fusion.71, ...), kind=kOutput, calls=%fused_computation.1 | convolution fusion | flops 644087808 | bytes 43778048 | tf_op jit(solution)/shard_map/dot_general | solution.py:18
  464.5 5.8 fusion.61
  470.3 1.4 fusion.60
  472.2 7.9 fusion.131
  480.2 7.8 fusion.133
  489.0 7.9 fusion.127
  497.0 8.0 fusion.129
  510.6 1.4 fusion.64
  512.0 2.9 convolution_add_fusion.2
  514.9 2.2 fusion.3
  518.5 2.3 fusion.2
  527.9 1.9 multiply_convert_fusion.7
  529.7 1.8 collective-permute-start.3
  535.8 1.7 multiply_convert_fusion.10
  539.9 3.1 collective-permute-done.2
  543.0 3.8 multiply_convert_fusion.11
  553.7 1.8 fusion.4
  556.1 1.4 convolution_add_fusion.13
  557.8 273.4 %all-reduce.7.cloned.1.call-done = (f32[1024,128]{1,0:T(8,128)}, f32[128,3072]{1,0:T(8,128)}, f32[1024,128]{1,0:T(8,128)}, f32[128,1024]{1,0:T(8,128)}, f32[1024...) async-done(((f32[1024,128]{1,0:T(8,128)}, f32[128,3072]{1,0:T(8,128)}, ...) | async-done | bytes 11796496 | tf_op jit(solution)/shard_map/psum | solution.py:204
  831.3 9.1 fusion.122
  840.9 10.7 fusion.126
  852.0 1.5 pad_maximum_fusion.6
  855.5 3.5 add_multiply_fusion
  859.1 6.8 fusion.38
  867.1 1.5 pad_maximum_fusion.7
  868.6 192.0 %all-reduce.5.cloned.1.call-done = (f32[1024,128]{1,0:T(8,128)}, f32[128,3072]{1,0:T(8,128)}, f32[1024,128]{1,0:T(8,128)}, f32[128,1024]{1,0:T(8,128)}, f32[1024...) async-done(((f32[1024,128]{1,0:T(8,128)}, f32[128,3072]{1,0:T(8,128)}, ...) | async-done | bytes 11796496 | tf_op jit(solution)/shard_map/psum | solution.py:219
  1060.6 1.9 copy.53
  1062.5 2.8 copy.54
  1067.7 1.4 copy.58
  1070.6 1.4 copy.60
  1073.1 1.4 copy.61
  (401 shorter events, 63.0 us)
Async XLA Ops:
  7.2 367.0 %copy-start = (bf16[128,4608]{1,0:T(8,128)(2,1)S(1)}, bf16[128,4608]{1,0:T(8,128)(2,1)}, u32[]{:S(2)}) copy-start(bf16[128,4608]{1,0:T(8,128)(2,1)} %param.37) | copy-start | bytes 3538948
  7.2 67.7 %all-gather.6.cloned.1.call-start = ((), (), s32[]{:S(2)}) async-start(), calls=%async_computation | async-start | bytes 6684672 | tf_op jit(solution)/shard_map/all_gather | solution.py:104
  7.9 8.1 copy-start.18
  8.0 8.1 copy-start.70
  8.0 109.1 %all-gather.8.cloned.1.call-start = ((), (), s32[]{:S(2)}) async-start(), calls=%async_computation.1 | async-start | bytes 2228224 | tf_op jit(solution)/shard_map/all_gather | solution.py:105
  8.7 190.9 %all-gather.12.cloned.1.call-start = ((), (), s32[]{:S(2)}) async-start(), calls=%async_computation.3 | async-start | bytes 10027008 | tf_op jit(solution)/shard_map/all_gather | solution.py:107
  9.5 271.9 %all-gather.14.cloned.1.call-start = ((), (), s32[]{:S(2)}) async-start(), calls=%async_computation.4 | async-start | bytes 10027008 | tf_op jit(solution)/shard_map/all_gather | solution.py:108
  10.0 353.1 %all-gather.10.cloned.1.call-start = ((), (), s32[]{:S(2)}) async-start(), calls=%async_computation.2 | async-start | bytes 10027008 | tf_op jit(solution)/shard_map/all_gather | solution.py:106
  10.6 820.6 %all-reduce.7.cloned.1.call-start = ((), (), s32[]{:S(2)}) async-start(), calls=%async_computation.6 | async-start | bytes 23592960 | tf_op jit(solution)/shard_map/psum | solution.py:204
  10.7 75.1 %copy-start.115 = (f32[1024]{0:T(1024)}, f32[1024]{0:T(1024)S(1)}, u32[]{:S(2)}) copy-start(f32[1024]{0:T(1024)S(1)} %convert_element_type.169) | copy-start | bytes 12292
  11.9 6.8 copy-start.127
  16.0 58.9 %copy-start.111 = (f32[512]{0:T(512)}, f32[512]{0:T(512)S(1)}, u32[]{:S(2)}) copy-start(f32[512]{0:T(512)S(1)} %add_rsqrt_fusion.1) | copy-start | bytes 6148
  16.1 69.7 %copy-start.113 = (f32[512]{0:T(512)}, f32[512]{0:T(512)S(1)}, u32[]{:S(2)}) copy-start(f32[512]{0:T(512)S(1)} %add_rsqrt_fusion.3) | copy-start | bytes 6148
  18.8 62.0 %copy-start.91 = (bf16[512,128]{1,0:T(8,128)(2,1)}, bf16[512,128]{1,0:T(8,128)(2,1)S(1)}, u32[]{:S(2)}) copy-start(bf16[512,128]{1,0:T(8,128)(2,1)S(1)} %fusion.69) | copy-start | bytes 393220
  18.8 56.1 %copy-start.24 = (bf16[2,1,512,1024]{3,2,1,0:T(8,128)(2,1)S(1)}, bf16[2,1,512,1024]{3,2,1,0:T(8,128)(2,1)}, u32[]{:S(2)}) copy-start(bf16[2,1,512,1024]{3,2,1,0:T(8,128)(2,1)} %param.21) | copy-start | bytes 6291460
  19.3 70.1 %copy-start.93 = (bf16[512,128]{1,0:T(8,128)(2,1)}, bf16[512,128]{1,0:T(8,128)(2,1)S(1)}, u32[]{:S(2)}) copy-start(bf16[512,128]{1,0:T(8,128)(2,1)S(1)} %fusion.65) | copy-start | bytes 393220
  74.9 5.9 copy-start.41
  74.9 10.9 %slice-start.18 = ((s8[6291456]{0:T(1024)(128)(4,1)}), s8[4194304]{0:T(1024)(128)(4,1)S(1)}, s32[]{:S(2)}) async-start(s8[6291456]{0:T(1024)(128)(4,1)} %bitcast.241), calls=%async_computation.25 | async-start | bytes 8388608
  81.8 11.9 %copy-start.2 = (f32[512,3072]{1,0:T(8,128)}, f32[512,3072]{1,0:T(8,128)S(1)}, u32[]{:S(2)}) copy-start(f32[512,3072]{1,0:T(8,128)S(1)} %multiply_add_fusion.4) | copy-start | bytes 18874372
  82.4 10.2 collective-permute-start.1
  91.0 2.7 collective-permute-start
  92.6 30.3 %copy-start.98 = (f32[1024]{0:T(1024)}, f32[1024]{0:T(1024)S(1)}, u32[]{:S(2)}) copy-start(f32[1024]{0:T(1024)S(1)} %convert_element_type.175) | copy-start | bytes 12292
  124.2 313.1 %copy-start.16 = (bf16[512,1024]{1,0:T(8,128)(2,1)}, bf16[512,1024]{1,0:T(8,128)(2,1)S(1)}, u32[]{:S(2)}) copy-start(bf16[512,1024]{1,0:T(8,128)(2,1)S(1)} %get-tuple-element.66) | copy-start | bytes 3145732
  126.2 293.2 %copy-start.49 = (bf16[512,128]{1,0:T(8,128)(2,1)}, bf16[512,128]{1,0:T(8,128)(2,1)S(1)}, u32[]{:S(2)}) copy-start(bf16[512,128]{1,0:T(8,128)(2,1)S(1)} %fusion.72) | copy-start | bytes 393220
  199.6 7.7 copy-start.29
  281.4 8.3 copy-start.31
  281.4 8.3 copy-start.76
  392.8 7.4 slice-start.10
  396.3 7.6 slice-start.14
  403.9 6.7 copy-start.78
  424.3 8.0 copy-start.32
  424.3 8.0 copy-start.74
  448.3 16.2 %copy-start.121 = (f32[128]{0:T(128)S(1)}, f32[128]{0:T(128)}, u32[]{:S(2)}) copy-start(f32[128]{0:T(128)} %copy-done.120) | copy-start | bytes 1540
  464.5 7.6 copy-start.13
  471.7 8.3 slice-start.6
  472.2 7.9 slice-start.7
  472.2 16.8 %slice-start.16 = ((s8[4718592]{0:T(1024)(128)(4,1)}), s8[4194304]{0:T(1024)(128)(4,1)S(1)}, s32[]{:S(2)}) async-start(s8[4718592]{0:T(1024)(128)(4,1)} %bitcast.233), calls=%async_computation.23 | async-start | bytes 8388608
  480.1 7.8 copy-start.5
  480.1 7.8 copy-start.67
  480.1 7.8 copy-start.99
  480.1 7.8 copy-start.107
  480.1 8.8 slice-start.17
  488.0 8.9 slice-start.12
  489.0 7.9 slice-start.13
  496.9 8.0 copy-start.7
  496.9 8.0 copy-start.27
  496.9 8.0 copy-start.79
  496.9 8.0 copy-start.109
  507.7 16.9 %copy-start.11 = (f32[512,1024]{1,0:T(8,128)}, f32[512,1024]{1,0:T(8,128)S(1)}, u32[]{:S(2)}) copy-start(f32[512,1024]{1,0:T(8,128)S(1)} %get-tuple-element.55) | copy-start | bytes 6291460
  507.7 25.1 %copy-start.9 = (f32[512,1024]{1,0:T(8,128)}, f32[512,1024]{1,0:T(8,128)S(1)}, u32[]{:S(2)}) copy-start(f32[512,1024]{1,0:T(8,128)S(1)} %get-tuple-element.54) | copy-start | bytes 6291460
  512.0 6.5 slice-start.4
  527.9 6.8 slice-start.2
  529.7 10.2 collective-permute-start.3
  537.5 5.6 copy-start.101
  537.5 5.6 copy-start.103
  537.5 5.6 copy-start.105
  537.5 5.5 collective-permute-start.2
  557.6 503.0 %all-reduce.5.cloned.1.call-start = ((), (), s32[]{:S(2)}) async-start(), calls=%async_computation.5 | async-start | bytes 23592960 | tf_op jit(solution)/shard_map/psum | solution.py:219
  831.3 9.2 copy-start.8
  831.3 9.2 copy-start.71
  840.4 14.0 %slice-start.20 = ((s8[6291456]{0:T(1024)(128)(4,1)}), s8[4194304]{0:T(1024)(128)(4,1)S(1)}, s32[]{:S(2)}) async-start(s8[6291456]{0:T(1024)(128)(4,1)} %bitcast.243), calls=%async_computation.27 | async-start | bytes 8388608
  840.9 13.6 %slice-start.21 = ((s8[6291456]{0:T(1024)(128)(4,1)}), s8[2097152]{0:T(1024)(128)(4,1)S(1)}, s32[]{:S(2)}) async-start(s8[6291456]{0:T(1024)(128)(4,1)} %bitcast.243), calls=%async_computation.28 | async-start | bytes 4194304
  859.1 6.9 copy-start.10
  859.1 6.9 copy-start.12
  (98 other events, 243.1 us)
Sparse Core Ops, SparseCore 0:
  10.3 64.5 all-gather.5
  77.1 39.9 all-gather.7
  119.4 80.2 all-gather.11
  201.8 79.5 all-gather.13
  283.5 79.5 all-gather.9
  557.7 273.4 all-reduce.6
  836.2 224.3 all-reduce.4
